TPU v7x, 256 devices: a whole 4x4x8 slice. The times are simulated.
256 devices in a mesh: dp: 32 (over z, y), row: 2 (over core), col: 4 (over x).
Axes of the slice: x: 4, y: 4, z: 8, core: 2. Of those that a mesh axis runs over, the one named last changes fastest.
Arguments:
- x_input: bfloat16 [32, 32, 64, 640], P('dp', 'row', 'col'), may hold values from -6 to 6
- pre_act: bfloat16 [32, 32, 64, 640], P('dp', 'row', 'col'), may hold values from -6 to 6
- out_grad: bfloat16 [32, 32, 64, 640], P('dp', 'row', 'col'), may hold values from -0.15625 to 0.15625
- conv_weight: bfloat16 [3, 3, 640, 640], replicated, may hold values from -0.078125 to 0.078125
- q_prev: float32 [5760, 2, 64], replicated, may hold values from -6 to 6
Outputs:
- p_basis: float32 [640, 2, 64], P('dp')
- q_next: float32 [5760, 2, 64], P('dp')
All inputs are finite; a program needn't handle non-finite values.
Results may differ from a plain program's by a relative error of at most 0.0036.
Values may be sent and summed in bfloat16 or wider, within the bound.
A program may use at most 128 MiB of HBM per device.

v0:
```python
import jax
import jax.numpy as jnp
from jax import lax
from jax.sharding import PartitionSpec as P


def padded_2(value, sides, width):
    for axis, dim in sides:
        size, length = (lax.axis_size(axis), value.shape[dim])
        up = [(i, (i + 1) % size) for i in range(size - 1)]
        down = [(j, i) for i, j in up]
        last = lax.slice_in_dim(value, length - width, length, axis=dim)
        leading = lax.slice_in_dim(value, 0, width, axis=dim)
        before = lax.ppermute(last, axis, up)
        after = lax.ppermute(leading, axis, down)
        value = jnp.concatenate([before, value, after], axis=dim)
    return value


def silu_slope(pre_float):
    sigma = jax.nn.sigmoid(pre_float)
    return sigma * (1.0 + pre_float * (1.0 - sigma))


def contract_first(left, right, exact):
    if exact:
        return lax.dot_general(
            left,
            right,
            (((0,), (0,)), ((), ())),
            precision=lax.Precision.HIGHEST,
            preferred_element_type=jnp.float32,
        )
    return lax.dot_general(
        left, right, (((0,), (0,)), ((), ())), preferred_element_type=jnp.float32
    )


def tap_window(padded, shift_row, shift_col, height, breadth):
    return padded[
        1 + shift_row : 1 + shift_row + height, 1 + shift_col : 1 + shift_col + breadth, :
    ].reshape(height * breadth, padded.shape[2])


def column_terms(moments, q_prev):
    return jnp.stack(
        [contract_first(moments[layer], q_prev[:, layer, :], True) for layer in range(2)], axis=1
    )


def row_terms(moments, ortho_basis):
    return jnp.stack(
        [
            jnp.dot(
                moments[layer],
                ortho_basis[:, layer, :],
                precision=lax.Precision.HIGHEST,
                preferred_element_type=jnp.float32,
            )
            for layer in range(2)
        ],
        axis=1,
    )


def gram_of(power_raw):
    return jnp.einsum(
        "mqn,mqg->qng",
        power_raw,
        power_raw,
        precision=lax.Precision.HIGHEST,
        preferred_element_type=jnp.float32,
    )


def orthonormal(power_raw, gram_matrix):
    bases = []
    for layer in range(2):
        lower = jnp.linalg.cholesky(gram_matrix[layer])
        bases.append(
            lax.linalg.triangular_solve(
                lower, power_raw[:, layer, :], left_side=False, lower=True, transpose_a=True
            )
        )
    return jnp.stack(bases, axis=1)


def on_device(x_input, pre_act, out_grad, conv_weight, q_prev):
    height, breadth, channels = (x_input.shape[1], x_input.shape[2], x_input.shape[3])
    pixels = height * breadth
    input_tile = x_input.reshape(height, breadth, channels)
    grad_tile = out_grad.reshape(height, breadth, channels)
    pre_float = pre_act.reshape(pixels, channels).astype(jnp.float32)
    hidden_flat = jax.nn.silu(pre_float).astype(jnp.bfloat16)
    grad_pad = padded_2(grad_tile, (("row", 0), ("col", 1)), 1)
    back_grad = jnp.zeros((pixels, channels), jnp.float32)
    second_taps = []
    for shift_row in (-1, 0, 1):
        for shift_col in (-1, 0, 1):
            window = tap_window(grad_pad, -shift_row, -shift_col, height, breadth)
            back_grad = back_grad + lax.dot_general(
                window,
                conv_weight[shift_row + 1, shift_col + 1],
                (((1,), (1,)), ((), ())),
                preferred_element_type=jnp.float32,
            )
            second_taps.append(contract_first(hidden_flat, window, False))
    pre_grad = (back_grad * silu_slope(pre_float)).astype(jnp.bfloat16)
    first_taps = []
    deriv_pad = padded_2(pre_grad.reshape(height, breadth, channels), (("row", 0), ("col", 1)), 1)
    input_flat = input_tile.reshape(pixels, channels)
    for shift_row in (-1, 0, 1):
        for shift_col in (-1, 0, 1):
            first_taps.append(
                contract_first(
                    input_flat,
                    tap_window(deriv_pad, -shift_row, -shift_col, height, breadth),
                    False,
                )
            )
    moments = jnp.stack(
        [
            jnp.stack(first_taps).reshape(9 * channels, channels),
            jnp.stack(second_taps).reshape(9 * channels, channels),
        ]
    )
    kernel_rows = moments.shape[1]
    owner = lax.axis_index("dp")
    basis_count = channels // lax.axis_size("dp")
    factor_count = kernel_rows // lax.axis_size("dp")
    power_raw = column_terms(moments, q_prev)
    for axis in ("row", "col", "dp"):
        power_raw = lax.psum(power_raw, axis)
    ortho_basis = orthonormal(power_raw, gram_of(power_raw))
    factor_out = lax.psum_scatter(
        row_terms(moments, ortho_basis), "dp", scatter_dimension=0, tiled=True
    )
    for axis in ("row", "col"):
        factor_out = lax.psum(factor_out, axis)
    basis_out = lax.dynamic_slice_in_dim(ortho_basis, owner * basis_count, basis_count, 0)
    return (basis_out, factor_out)


def solution(mesh):
    placed = (
        P("dp", "row", "col", None),
        P("dp", "row", "col", None),
        P("dp", "row", "col", None),
        P(),
        P(),
    )
    return jax.shard_map(
        on_device,
        mesh=mesh,
        in_specs=placed,
        out_specs=(P("dp", None, None), P("dp", None, None)),
        check_vma=False,
    )
```

profile of v0, /device:TPU:8, one launch (start us, length us, event | category | flops | bytes accessed | tf_op | source)
XLA Modules:
  0.0 609.8 jit_solution(7711296566547497687)
XLA Ops:
  8.0 1.3 collective-permute-start.1
  9.3 3.0 collective-permute-start
  12.3 1.2 fusion.43
  15.8 3.4 collective-permute-start.3
  19.2 1.3 collective-permute-start.2
  21.7 1.6 fusion.23
  23.3 1.9 collective-permute-done.2
  25.2 1.3 maximum_maximum_fusion
  37.1 1.4 collective-permute-start.5
  38.5 3.2 collective-permute-start.4
  41.7 8.8 %fusion.12 = f32[640,1,64]{0,2,1:T(8,128)S(1)} fusion(f32[5760,640]{1,0:T(8,128)S(1)} %bitcast.256, f32[5760,2,64]{0,2,1:T(8,128)S(1)} %copy-done.6), kind=kOutput, calls=%fused_computation.38 | convolution fusion | flops 2831155200 | bytes 16384000 | tf_op jit(solution)/shard_map/dot_general | solution.py:27
  50.7 3.4 collective-permute-start.7
  54.1 1.5 collective-permute-start.6
  55.8 4.2 collective-permute-done.6
  64.7 9.3 %fusion.9 = f32[640,1,64]{0,2,1:T(8,128)S(1)} fusion(f32[5760,640]{1,0:T(8,128)S(1)} %bitcast.252, f32[5760,2,64]{0,2,1:T(8,128)S(1)} %copy-done.6), kind=kOutput, calls=%fused_computation.37 | convolution fusion | flops 2831155200 | bytes 16384000 | tf_op jit(solution)/shard_map/dot_general | solution.py:27
  74.8 31.2 %all-reduce.8.cloned.1.call-done = f32[640,2,64]{0,2,1:T(8,128)} async-done(((f32[640,2,64]{0,2,1:T(8,128)}), f32[640,2,64]{0,2,1:T(8,128)}) %all-reduce.8.cloned.1.call-update) | async-done | bytes 327696 | tf_op jit(solution)/shard_map/psum | solution.py:133
  106.1 50.8 %all-reduce.10.cloned.1.call-done = f32[640,2,64]{0,2,1:T(8,128)} async-done(((f32[640,2,64]{0,2,1:T(8,128)}), f32[640,2,64]{0,2,1:T(8,128)}) %all-reduce.10.cloned.1.call-update) | async-done | bytes 327696 | tf_op jit(solution)/shard_map/psum | solution.py:133
  156.9 148.6 %all-reduce.12.cloned.1.call-done = f32[640,2,64]{0,2,1:T(8,128)} async-done(((f32[640,2,64]{0,2,1:T(8,128)}), f32[640,2,64]{0,2,1:T(8,128)}) %all-reduce.12.cloned.1.call-update) | async-done | bytes 327696 | tf_op jit(solution)/shard_map/psum | solution.py:133
  305.6 1.5 fusion.62
  307.3 5.8 cholesky.44
  314.5 4.9 custom-call.6
  319.4 5.9 cholesky.55
  326.6 4.9 custom-call.7
  331.5 1.4 fusion.45
  332.9 17.3 %convolution_bitcast_fusion = f32[5760,1,64]{0,2,1:T(8,128)S(1)} fusion(f32[5760,640]{1,0:T(8,128)} %bitcast.257, f32[64,640]{1,0:T(8,128)S(1)} %fusion.45), kind=kOutput, calls=%fused_computation | convolution fusion | flops 2831155200 | bytes 16384000 | tf_op jit(solution)/shard_map/dot_general | solution.py:54
  350.7 14.2 %convolution_bitcast_fusion.1 = f32[5760,1,64]{0,2,1:T(8,128)S(1)} fusion(f32[5760,640]{1,0:T(8,128)S(1)} %bitcast.255, f32[64,640]{1,0:T(8,128)S(1)} %fusion.46), kind=kOutput, calls=%fused_computation.1 | convolution fusion | flops 2831155200 | bytes 16384000 | tf_op jit(solution)/shard_map/dot_general | solution.py:54
  364.9 1.8 pad_maximum_fusion
  368.0 153.1 %all-reduce.18.cloned.1.call-done = f32[5760,2,64]{0,2,1:T(8,128)} async-done(((f32[5760,2,64]{0,2,1:T(8,128)}), f32[5760,2,64]{0,2,1:T(8,128)}) %all-reduce.18.cloned.1.call-update) | async-done | bytes 2949136
  521.1 1.7 constant_dynamic-slice_fusion
  522.9 28.5 %all-reduce.14.cloned.1.call-done = f32[180,2,64]{0,2,1:T(8,128)} async-done(((f32[180,2,64]{0,2,1:T(8,128)}), f32[180,2,64]{0,2,1:T(8,128)}) %all-reduce.14.cloned.1.call-update) | async-done | bytes 92176 | tf_op jit(solution)/shard_map/psum | solution.py:139
  552.1 49.0 %all-reduce.16.cloned.1.call-done = f32[180,2,64]{0,2,1:T(8,128)} async-done(((f32[180,2,64]{0,2,1:T(8,128)}), f32[180,2,64]{0,2,1:T(8,128)}) %all-reduce.16.cloned.1.call-update) | async-done | bytes 92176 | tf_op jit(solution)/shard_map/psum | solution.py:139
  601.2 1.6 copy.42
  (102 shorter events, 25.2 us)
Async XLA Ops:
  7.2 53.4 %copy-start = (bf16[1,16,16,640]{3,2,1,0:T(8,128)(2,1)S(1)}, bf16[1,16,16,640]{3,2,1,0:T(8,128)(2,1)}, u32[]{:S(2)}) copy-start(bf16[1,16,16,640]{3,2,1,0:T(8,128)(2,1)} %param.8) | copy-start | bytes 983044
  7.2 98.8 %all-reduce.8.cloned.1.call-start = ((), (), s32[]{:S(2)}) async-start(), calls=%async_computation | async-start | bytes 655360 | tf_op jit(solution)/shard_map/psum | solution.py:133
  8.0 6.7 %collective-permute-start.1 = (bf16[1,16,640]{2,1,0:T(8,128)(2,1)S(1)}, bf16[1,16,640]{2,1,0:T(8,128)(2,1)S(1)}, u32[]{:S(2)}, u32[]{:S(2)}) collective-permute-start(bf16[1,16,640]{2,1,0:T(8,128)(2,1)S(1)} %get-tuple-element.35), channel_id=1, source_target_pairs={{4,0},{5,1},{6,2},{7,3},{12,8},{13,9},{14,10},{15,11},{20,16},{21,... | collective-permute-start | bytes 61448 | tf_op jit(solution)/shard_map/ppermute | solution.py:15
  9.3 5.4 collective-permute-start
  15.8 7.5 %collective-permute-start.3 = (bf16[18,1,640]{2,1,0:T(2,128)(2,1)S(1)}, bf16[18,1,640]{2,1,0:T(2,128)(2,1)S(1)}, u32[]{:S(2)}, u32[]{:S(2)}) collective-permute-start(bf16[18,1,640]{2,1,0:T(2,128)(2,1)S(1)} %get-tuple-element.26), channel_id=1, source_target_pairs={{0,1},{1,2},{2,3},{4,5},{5,6},{6,7},{8,9},{9,10},{10,11},{12,13},{... | collective-permute-start | bytes 69128 | tf_op jit(solution)/shard_map/ppermute | solution.py:14
  19.2 6.0 collective-permute-start.2
  23.3 5.3 copy-start.4
  23.3 5.3 copy-start.7
  28.1 2.2 slice-start.4
  28.6 2.8 slice-start.5
  33.7 8.0 %copy-start.3 = (f32[9,640,640]{2,1,0:T(8,128)}, f32[9,640,640]{2,1,0:T(8,128)S(1)}, u32[]{:S(2)}) copy-start(f32[9,640,640]{2,1,0:T(8,128)S(1)} %bitcast_dynamic-update-slice_fusion.9) | copy-start | bytes 44236804
  34.2 7.5 %copy-start.6 = (f32[5760,2,64]{0,2,1:T(8,128)S(1)}, f32[5760,2,64]{0,2,1:T(8,128)}, u32[]{:S(2)}) copy-start(f32[5760,2,64]{0,2,1:T(8,128)} %param.12) | copy-start | bytes 8847364
  37.1 13.5 %collective-permute-start.5 = (bf16[1,16,640]{2,1,0:T(8,128)(2,1)S(1)}, bf16[1,16,640]{2,1,0:T(8,128)(2,1)S(1)}, u32[]{:S(2)}, u32[]{:S(2)}) collective-permute-start(bf16[1,16,640]{2,1,0:T(8,128)(2,1)S(1)} %get-tuple-element.31), channel_id=1, source_target_pairs={{4,0},{5,1},{6,2},{7,3},{12,8},{13,9},{14,10},{15,11},{20,16},{21,... | collective-permute-start | bytes 61448 | tf_op jit(solution)/shard_map/ppermute | solution.py:15
  38.5 12.1 %collective-permute-start.4 = (bf16[1,16,640]{2,1,0:T(8,128)(2,1)S(1)}, bf16[1,16,640]{2,1,0:T(8,128)(2,1)S(1)}, u32[]{:S(2)}, u32[]{:S(2)}) collective-permute-start(bf16[1,16,640]{2,1,0:T(8,128)(2,1)S(1)} %get-tuple-element.30), channel_id=1, source_target_pairs={{0,4},{1,5},{2,6},{3,7},{8,12},{9,13},{10,14},{11,15},{16,20},{17,... | collective-permute-start | bytes 61448 | tf_op jit(solution)/shard_map/ppermute | solution.py:14
  50.7 5.1 collective-permute-start.7
  54.1 6.0 collective-permute-start.6
  64.7 9.3 %copy-start.2 = (f32[9,640,640]{2,1,0:T(8,128)}, f32[9,640,640]{2,1,0:T(8,128)S(1)}, u32[]{:S(2)}) copy-start(f32[9,640,640]{2,1,0:T(8,128)S(1)} %bitcast_dynamic-update-slice_fusion) | copy-start | bytes 44236804
  74.8 82.1 %all-reduce.10.cloned.1.call-start = ((), (), s32[]{:S(2)}) async-start(), calls=%async_computation.1 | async-start | bytes 655360 | tf_op jit(solution)/shard_map/psum | solution.py:133
  106.0 199.5 %all-reduce.12.cloned.1.call-start = ((), (), s32[]{:S(2)}) async-start(), calls=%async_computation.2 | async-start | bytes 655360 | tf_op jit(solution)/shard_map/psum | solution.py:133
  156.9 364.2 %all-reduce.18.cloned.1.call-start = ((), (), s32[]{:S(2)}) async-start(), calls=%async_computation.5 | async-start | bytes 5898240
  331.5 19.1 %slice-start = ((s8[14745600]{0:T(1024)(128)(4,1)}), s8[4194304]{0:T(1024)(128)(4,1)S(1)}, s32[]{:S(2)}) async-start(s8[14745600]{0:T(1024)(128)(4,1)} %bitcast.253), calls=%async_computation.6 | async-start | bytes 8388608
  332.9 17.3 %copy-start.5 = (f32[640,2,64]{0,2,1:T(8,128)S(1)}, f32[640,2,64]{0,2,1:T(8,128)}, u32[]{:S(2)}) copy-start(f32[640,2,64]{0,2,1:T(8,128)} %all-reduce.12.cloned.1.call-done) | copy-start | bytes 983044
  332.9 17.7 %slice-start.1 = ((s8[14745600]{0:T(1024)(128)(4,1)}), s8[4194304]{0:T(1024)(128)(4,1)S(1)}, s32[]{:S(2)}) async-start(s8[14745600]{0:T(1024)(128)(4,1)} %bitcast.253), calls=%async_computation.7 | async-start | bytes 8388608
  332.9 17.7 %slice-start.2 = ((s8[14745600]{0:T(1024)(128)(4,1)}), s8[4194304]{0:T(1024)(128)(4,1)S(1)}, s32[]{:S(2)}) async-start(s8[14745600]{0:T(1024)(128)(4,1)} %bitcast.253), calls=%async_computation.8 | async-start | bytes 8388608
  332.9 17.7 %slice-start.3 = ((s8[14745600]{0:T(1024)(128)(4,1)}), s8[2162688]{0:T(1024)(128)(4,1)S(1)}, s32[]{:S(2)}) async-start(s8[14745600]{0:T(1024)(128)(4,1)} %bitcast.253), calls=%async_computation.9 | async-start | bytes 4325376
  350.7 252.1 %copy-start.1 = (bf16[1,16,16,640]{3,2,1,0:T(8,128)(2,1)S(1)}, bf16[1,16,16,640]{3,2,1,0:T(8,128)(2,1)}, u32[]{:S(2)}) copy-start(bf16[1,16,16,640]{3,2,1,0:T(8,128)(2,1)} %param.8) | copy-start | bytes 983044
  364.9 1.9 copy-start.8
  366.7 184.6 %all-reduce.14.cloned.1.call-start = ((), (), s32[]{:S(2)}) async-start(), calls=%async_computation.3 | async-start | bytes 262144 | tf_op jit(solution)/shard_map/psum | solution.py:139
  522.8 78.4 %all-reduce.16.cloned.1.call-start = ((), (), s32[]{:S(2)}) async-start(), calls=%async_computation.4 | async-start | bytes 262144 | tf_op jit(solution)/shard_map/psum | solution.py:139
Sparse Core Ops, SparseCore 0:
  74.9 31.0 all-reduce.7
  108.5 48.3 all-reduce.9
  160.7 144.8 all-reduce.11
  366.9 154.2 all-reduce.17
  524.3 27.0 all-reduce.13
  553.6 47.5 all-reduce.15
where the time goes:
time: 616 us; the launch traced here: 610 us
  waiting for transfers between devices  468 us (76%)
  matrix products  66.6 us (11%)
  other arithmetic  33.1 us (5%)
  starting transfers between devices  18.8 us (3%)
  between operations  15.6 us (3%)
  local copies, waits for them, and re-layouts  8.22 us (1%)
    psum x3, waiting for transfers between devices, on_device(): power_raw = lax.psum(power_raw, axis)  231 us
    unnamed x7, waiting for transfers between devices  153 us
    psum x2, waiting for transfers between devices, on_device(): factor_out = lax.psum(factor_out, axis)  77.5 us
    dot_general x2, matrix products, row_terms(): jnp.dot(moments[layer], ortho_basis[:, layer, :], precision=lax.Precision...  31.5 us
    dot_general x2, matrix products, contract_first(): lax.dot_general(left, right, (((0,), (0,)), ((), ())), precision=lax.Prec...  18.1 us
    another operation x6, other arithmetic, orthonormal(): lower = jnp.linalg.cholesky(gram_matrix[layer])  13.1 us
    ppermute x4, starting transfers between devices, padded_2(): before = lax.ppermute(last, axis, up)  13 us
  transfers between devices with their start and end apart: 14, of which 9 were waited for; matrix products, arithmetic and copies ran while one was open for 3% of the time, Pallas kernels for 0%

commit v1 on v0

--- a/solution.py
+++ b/solution.py
@@ -130,7 +130,7 @@
     factor_count = kernel_rows // lax.axis_size("dp")
     power_raw = column_terms(moments, q_prev)
     for axis in ("row", "col", "dp"):
-        power_raw = lax.psum(power_raw, axis)
+        power_raw = jnp.sum(lax.all_gather(power_raw, axis), axis=0)
     ortho_basis = orthonormal(power_raw, gram_of(power_raw))
     factor_out = lax.psum_scatter(
         row_terms(moments, ortho_basis), "dp", scatter_dimension=0, tiled=True

time: 616 us -> 540 us (0.88)
  waiting for transfers between devices: 468 us -> 373 us
  local copies, waits for them, and re-layouts: 8.22 us -> 17.8 us
  other arithmetic: 33.1 us -> 41.1 us
    psum x3 -> x0, waiting for transfers between devices: 231 us -> none  [on_device(): power_raw = lax.psum(power_raw, axis)]
    all_gather x0 -> x2, waiting for transfers between devices: none -> 140 us  [on_device(): power_raw = jnp.sum(lax.all_gather(power_raw, axis), axis=0)]
    reduce_sum x0 -> x3, other arithmetic: none -> 8.7 us  [on_device(): power_raw = jnp.sum(lax.all_gather(power_raw, axis), axis=0)]
    unnamed x34 -> x23, local copies, waits for them, and re-layouts: 6.87 us -> 14.2 us
    unnamed x7 -> x6, waiting for transfers between devices: 153 us -> 153 us
  transfers between devices with their start and end apart: 14 -> 13, of which waited for: 9 -> 7; matrix products, arithmetic and copies ran while one was open for 3% -> 4% of each run, Pallas kernels for 0% -> 0%
where the time goes in v1:
time: 540 us; the launch traced here: 536 us
  waiting for transfers between devices  373 us (69%)
  matrix products  67.2 us (12%)
  other arithmetic  41.1 us (8%)
  starting transfers between devices  19.3 us (4%)
  local copies, waits for them, and re-layouts  17.8 us (3%)
  between operations  15.2 us (3%)
    unnamed x6, waiting for transfers between devices  153 us
    all_gather x2, waiting for transfers between devices, on_device(): power_raw = jnp.sum(lax.all_gather(power_raw, axis), axis=0)  140 us
    psum x2, waiting for transfers between devices, on_device(): factor_out = lax.psum(factor_out, axis)  77.5 us
    dot_general x2, matrix products, row_terms(): jnp.dot(moments[layer], ortho_basis[:, layer, :], precision=lax.Precision...  34.1 us
    dot_general x2, matrix products, contract_first(): lax.dot_general(left, right, (((0,), (0,)), ((), ())), precision=lax.Prec...  18.1 us
    unnamed x23, local copies, waits for them, and re-layouts  14.2 us
    ppermute x4, starting transfers between devices, padded_2(): before = lax.ppermute(last, axis, up)  13.8 us
    another operation x6, other arithmetic, orthonormal(): lower = jnp.linalg.cholesky(gram_matrix[layer])  13 us
  transfers between devices with their start and end apart: 13, of which 7 were waited for; matrix products, arithmetic and copies ran while one was open for 4% of the time, Pallas kernels for 0%

profile of v1, /device:TPU:8, one launch (start us, length us, event | category | flops | bytes accessed | tf_op | source)
XLA Modules:
  0.0 535.6 jit_solution(1238776194112328869)
XLA Ops:
  8.1 2.0 collective-permute-start
  10.1 1.3 collective-permute-start.1
  14.9 1.3 collective-permute-start.2
  16.2 4.5 collective-permute-start.3
  21.9 1.6 fusion.23
  23.6 1.3 maximum_maximum_fusion
  28.9 2.5 collective-permute-start.4
  31.4 1.5 collective-permute-start.5
  37.3 8.8 %fusion.12 = f32[640,1,64]{0,2,1:T(8,128)S(1)} fusion(f32[5760,640]{1,0:T(8,128)S(1)} %bitcast.262, f32[5760,2,64]{0,2,1:T(8,128)S(1)} %copy-done.6), kind=kOutput, calls=%fused_computation.38 | convolution fusion | flops 2831155200 | bytes 16384000 | tf_op jit(solution)/shard_map/dot_general | solution.py:27
  47.6 4.8 collective-permute-start.7
  52.5 1.5 collective-permute-done.7
  58.8 9.2 %fusion.9 = f32[640,1,64]{0,2,1:T(8,128)S(1)} fusion(f32[5760,640]{1,0:T(8,128)S(1)} %bitcast.264, f32[5760,2,64]{0,2,1:T(8,128)S(1)} %copy-done.6), kind=kOutput, calls=%fused_computation.37 | convolution fusion | flops 2831155200 | bytes 16384000 | tf_op jit(solution)/shard_map/dot_general | solution.py:27
  68.0 2.3 all-gather
  70.7 1.6 reduce_sum.27
  72.3 31.4 %all-gather.6.cloned.1.call-done = f32[2560,2,64]{0,2,1:T(8,128)} async-done(((f32[640,2,64]{0,2,1:T(8,128)}), f32[2560,2,64]{0,2,1:T(8,128)}) %all-gather.6.cloned.1.call-update) | async-done | bytes 1310736 | tf_op jit(solution)/shard_map/all_gather | solution.py:133
  103.7 1.7 reshape.112
  105.5 1.5 reduce_sum.28
  107.1 108.6 %all-gather.8.cloned.1.call-done = f32[20480,2,64]{0,2,1:T(8,128)} async-done(((f32[640,2,64]{0,2,1:T(8,128)}), f32[20480,2,64]{0,2,1:T(8,128)}) %all-gather.8.cloned.1.call-update) | async-done | bytes 10485776 | tf_op jit(solution)/shard_map/all_gather | solution.py:133
  215.8 9.6 %copy.20 = f32[16,8,32,640]{3,2,1,0:T(8,128)} copy(f32[16,8,32,640]{3,1,2,0:T(8,128)} %bitcast.275) | data formatting | bytes 20971520
  225.4 5.6 %reduce_sum.29 = f32[640,2,64]{0,2,1:T(8,128)S(1)} reduce(f32[32,640,2,64]{1,0,3,2:T(8,128)} %bitcast.266, f32[]{:T(128)} %constant.41.clone.1), dimensions={0}, to_apply=%region_2.3 | reduce | flops 2539520 | bytes 10813444 | tf_op jit(solution)/shard_map/reduce_sum | solution.py:133
  231.7 5.8 %cholesky.44 = f32[64,64]{1,0:T(8,128)S(1)} custom-call(f32[64,64]{1,0:T(8,128)S(1)} %get-tuple-element.37), custom_call_target="Cholesky" | custom-call | tf_op jit(solution)/shard_map/jit(cholesky)/cholesky | solution.py:79
  238.8 4.9 custom-call.6
  244.1 17.1 %convolution_bitcast_fusion.1 = f32[5760,1,64]{0,2,1:T(8,128)S(1)} fusion(f32[5760,640]{1,0:T(8,128)} %bitcast.265, f32[64,640]{1,0:T(8,128)S(1)} %fusion.46), kind=kOutput, calls=%fused_computation.1 | convolution fusion | flops 2831155200 | bytes 16384000 | tf_op jit(solution)/shard_map/dot_general | solution.py:54
  261.3 5.8 %cholesky.55 = f32[64,64]{1,0:T(8,128)S(1)} custom-call(f32[64,64]{1,0:T(8,128)S(1)} %get-tuple-element.36), custom_call_target="Cholesky" | custom-call | tf_op jit(solution)/shard_map/jit(cholesky)/cholesky | solution.py:79
  268.4 4.9 custom-call.7
  273.7 17.0 %convolution_bitcast_fusion = f32[5760,1,64]{0,2,1:T(8,128)S(1)} fusion(f32[5760,640]{1,0:T(8,128)} %bitcast.263, f32[64,640]{1,0:T(8,128)S(1)} %fusion.45), kind=kOutput, calls=%fused_computation | convolution fusion | flops 2831155200 | bytes 16384000 | tf_op jit(solution)/shard_map/dot_general | solution.py:54
  290.7 1.8 pad_maximum_fusion
  293.9 153.3 %all-reduce.9.cloned.1.call-done = f32[5760,2,64]{0,2,1:T(8,128)} async-done(((f32[5760,2,64]{0,2,1:T(8,128)}), f32[5760,2,64]{0,2,1:T(8,128)}) %all-reduce.9.cloned.1.call-update) | async-done | bytes 2949136
  447.2 1.7 constant_dynamic-slice_fusion
  449.0 28.5 %all-reduce.5.cloned.1.call-done = f32[180,2,64]{0,2,1:T(8,128)} async-done(((f32[180,2,64]{0,2,1:T(8,128)}), f32[180,2,64]{0,2,1:T(8,128)}) %all-reduce.5.cloned.1.call-update) | async-done | bytes 92176 | tf_op jit(solution)/shard_map/psum | solution.py:139
  478.3 49.0 %all-reduce.7.cloned.1.call-done = f32[180,2,64]{0,2,1:T(8,128)} async-done(((f32[180,2,64]{0,2,1:T(8,128)}), f32[180,2,64]{0,2,1:T(8,128)}) %all-reduce.7.cloned.1.call-update) | async-done | bytes 92176 | tf_op jit(solution)/shard_map/psum | solution.py:139
  527.3 1.6 copy.41
  (92 shorter events, 26.1 us)
Async XLA Ops:
  7.2 47.4 %copy-start = (bf16[1,16,16,640]{3,2,1,0:T(8,128)(2,1)S(1)}, bf16[1,16,16,640]{3,2,1,0:T(8,128)(2,1)}, u32[]{:S(2)}) copy-start(bf16[1,16,16,640]{3,2,1,0:T(8,128)(2,1)} %param.8) | copy-start | bytes 983044
  7.2 96.6 %all-gather.6.cloned.1.call-start = ((), (), s32[]{:S(2)}) async-start(), calls=%async_computation.2 | async-start | bytes 1638400 | tf_op jit(solution)/shard_map/all_gather | solution.py:133
  7.2 17.9 %copy-start.4 = (bf16[3,3,640,640]{3,2,1,0:T(8,128)(2,1)S(1)}, bf16[3,3,640,640]{3,2,1,0:T(8,128)(2,1)}, u32[]{:S(2)}) copy-start(bf16[3,3,640,640]{3,2,1,0:T(8,128)(2,1)} %param.11) | copy-start | bytes 22118404
  8.1 5.7 %collective-permute-start = (bf16[1,16,640]{2,1,0:T(8,128)(2,1)S(1)}, bf16[1,16,640]{2,1,0:T(8,128)(2,1)S(1)}, u32[]{:S(2)}, u32[]{:S(2)}) collective-permute-start(bf16[1,16,640]{2,1,0:T(8,128)(2,1)S(1)} %get-tuple-element.34), channel_id=1, source_target_pairs={{0,4},{1,5},{2,6},{3,7},{8,12},{9,13},{10,14},{11,15},{16,20},{17,... | collective-permute-start | bytes 61448 | tf_op jit(solution)/shard_map/ppermute | solution.py:14
  10.1 3.7 collective-permute-start.1
  14.9 8.6 %collective-permute-start.2 = (bf16[18,1,640]{2,1,0:T(2,128)(2,1)S(1)}, bf16[18,1,640]{2,1,0:T(2,128)(2,1)S(1)}, u32[]{:S(2)}, u32[]{:S(2)}) collective-permute-start(bf16[18,1,640]{2,1,0:T(2,128)(2,1)S(1)} %get-tuple-element.27), channel_id=1, source_target_pairs={{1,0},{2,1},{3,2},{5,4},{6,5},{7,6},{9,8},{10,9},{11,10},{13,12},{... | collective-permute-start | bytes 69128 | tf_op jit(solution)/shard_map/ppermute | solution.py:15
  16.2 7.3 %collective-permute-start.3 = (bf16[18,1,640]{2,1,0:T(2,128)(2,1)S(1)}, bf16[18,1,640]{2,1,0:T(2,128)(2,1)S(1)}, u32[]{:S(2)}, u32[]{:S(2)}) collective-permute-start(bf16[18,1,640]{2,1,0:T(2,128)(2,1)S(1)} %get-tuple-element.26), channel_id=1, source_target_pairs={{0,1},{1,2},{2,3},{4,5},{5,6},{6,7},{8,9},{9,10},{10,11},{12,13},{... | collective-permute-start | bytes 69128 | tf_op jit(solution)/shard_map/ppermute | solution.py:14
  23.5 3.5 copy-start.5
  27.9 6.9 %copy-start.7 = (bf16[1,16,16,640]{3,2,1,0:T(8,128)(2,1)S(1)}, bf16[1,16,16,640]{3,2,1,0:T(8,128)(2,1)}, u32[]{:S(2)}) copy-start(bf16[1,16,16,640]{3,2,1,0:T(8,128)(2,1)} %param.9) | copy-start | bytes 983044
  28.9 17.2 %collective-permute-start.4 = (bf16[1,16,640]{2,1,0:T(8,128)(2,1)S(1)}, bf16[1,16,640]{2,1,0:T(8,128)(2,1)S(1)}, u32[]{:S(2)}, u32[]{:S(2)}) collective-permute-start(bf16[1,16,640]{2,1,0:T(8,128)(2,1)S(1)} %get-tuple-element.30), channel_id=1, source_target_pairs={{0,4},{1,5},{2,6},{3,7},{8,12},{9,13},{10,14},{11,15},{16,20},{17,... | collective-permute-start | bytes 61448 | tf_op jit(solution)/shard_map/ppermute | solution.py:14
  31.4 14.7 %collective-permute-start.5 = (bf16[1,16,640]{2,1,0:T(8,128)(2,1)S(1)}, bf16[1,16,640]{2,1,0:T(8,128)(2,1)S(1)}, u32[]{:S(2)}, u32[]{:S(2)}) collective-permute-start(bf16[1,16,640]{2,1,0:T(8,128)(2,1)S(1)} %get-tuple-element.31), channel_id=1, source_target_pairs={{4,0},{5,1},{6,2},{7,3},{12,8},{13,9},{14,10},{15,11},{20,16},{21,... | collective-permute-start | bytes 61448 | tf_op jit(solution)/shard_map/ppermute | solution.py:15
  35.4 1.9 copy-start.6
  37.3 8.8 %copy-start.2 = (f32[9,640,640]{2,1,0:T(8,128)}, f32[9,640,640]{2,1,0:T(8,128)S(1)}, u32[]{:S(2)}) copy-start(f32[9,640,640]{2,1,0:T(8,128)S(1)} %bitcast_dynamic-update-slice_fusion.9) | copy-start | bytes 44236804
  46.3 6.3 %collective-permute-start.6 = (bf16[18,1,640]{2,1,0:T(2,128)(2,1)S(1)}, bf16[18,1,640]{2,1,0:T(2,128)(2,1)S(1)}, u32[]{:S(2)}, u32[]{:S(2)}) collective-permute-start(bf16[18,1,640]{2,1,0:T(2,128)(2,1)S(1)} %get-tuple-element.23), channel_id=1, source_target_pairs={{1,0},{2,1},{3,2},{5,4},{6,5},{7,6},{9,8},{10,9},{11,10},{13,12},{... | collective-permute-start | bytes 69128 | tf_op jit(solution)/shard_map/ppermute | solution.py:15
  47.6 6.5 %collective-permute-start.7 = (bf16[18,1,640]{2,1,0:T(2,128)(2,1)S(1)}, bf16[18,1,640]{2,1,0:T(2,128)(2,1)S(1)}, u32[]{:S(2)}, u32[]{:S(2)}) collective-permute-start(bf16[18,1,640]{2,1,0:T(2,128)(2,1)S(1)} %get-tuple-element.22), channel_id=1, source_target_pairs={{0,1},{1,2},{2,3},{4,5},{5,6},{6,7},{8,9},{9,10},{10,11},{12,13},{... | collective-permute-start | bytes 69128 | tf_op jit(solution)/shard_map/ppermute | solution.py:14
  58.8 9.2 %copy-start.3 = (f32[9,640,640]{2,1,0:T(8,128)}, f32[9,640,640]{2,1,0:T(8,128)S(1)}, u32[]{:S(2)}) copy-start(f32[9,640,640]{2,1,0:T(8,128)S(1)} %bitcast_dynamic-update-slice_fusion) | copy-start | bytes 44236804
  72.2 143.5 %all-gather.8.cloned.1.call-start = ((), (), s32[]{:S(2)}) async-start(), calls=%async_computation.3 | async-start | bytes 10813440 | tf_op jit(solution)/shard_map/all_gather | solution.py:133
  107.1 340.2 %all-reduce.9.cloned.1.call-start = ((), (), s32[]{:S(2)}) async-start(), calls=%async_computation.4 | async-start | bytes 5898240
  273.7 255.2 %copy-start.1 = (bf16[1,16,16,640]{3,2,1,0:T(8,128)(2,1)S(1)}, bf16[1,16,16,640]{3,2,1,0:T(8,128)(2,1)}, u32[]{:S(2)}) copy-start(bf16[1,16,16,640]{3,2,1,0:T(8,128)(2,1)} %param.8) | copy-start | bytes 983044
  290.7 1.9 copy-start.8
  292.6 184.9 %all-reduce.5.cloned.1.call-start = ((), (), s32[]{:S(2)}) async-start(), calls=%async_computation | async-start | bytes 262144 | tf_op jit(solution)/shard_map/psum | solution.py:139
  448.9 78.4 %all-reduce.7.cloned.1.call-start = ((), (), s32[]{:S(2)}) async-start(), calls=%async_computation.1 | async-start | bytes 262144 | tf_op jit(solution)/shard_map/psum | solution.py:139
Sparse Core Ops, SparseCore 0:
  72.4 31.3 all-gather.5
  107.2 108.5 all-gather.7
  292.7 154.4 all-reduce.8
  450.4 27.0 all-reduce.4
  479.8 47.5 all-reduce.6
